TPU v7x, 32 devices: a whole 2x2x4 slice. The times are simulated.
32 devices in a mesh: fsdp: 4 (over y, core), ctx: 2 (over x), tp: 4 (over z).
Axes of the slice: x: 2, y: 2, z: 4, core: 2. Of those that a mesh axis runs over, the one named last changes fastest.
Arguments:
- hidden_in: bfloat16 [4096, 2304], P(('fsdp', 'ctx')), may hold values from -36 to 36
- cotangent: bfloat16 [4096, 2304], P(('fsdp', 'ctx')), may hold values from -6 to 6
- segment_ids: int32 [4096], P('fsdp'), may hold values from -1 to 4, as said below
- pre_attention_gain: float32 [2304], replicated, may hold values from 0.25 to 1.75
- post_attention_gain: float32 [2304], replicated, may hold values from 0.25 to 1.75
- pre_feedforward_gain: float32 [2304], replicated, may hold values from 0.25 to 1.75
- post_feedforward_gain: float32 [2304], replicated, may hold values from 0.25 to 1.75
- query_weight: bfloat16 [2304, 2048], P(('fsdp', 'ctx'), 'tp'), may hold values from -0.3125 to 0.3125
- key_weight: bfloat16 [2304, 1024], P(('fsdp', 'ctx'), 'tp'), may hold values from -0.3125 to 0.3125
- value_weight: bfloat16 [2304, 1024], P(('fsdp', 'ctx'), 'tp'), may hold values from -0.125 to 0.125
- output_weight: bfloat16 [2304, 2048], P(('fsdp', 'ctx'), 'tp'), may hold values from -0.125 to 0.125
- gate_weight: bfloat16 [2304, 9216], P(('fsdp', 'ctx'), 'tp'), may hold values from -0.125 to 0.125
- up_weight: bfloat16 [2304, 9216], P(('fsdp', 'ctx'), 'tp'), may hold values from -0.125 to 0.125
- down_weight: bfloat16 [2304, 9216], P(('fsdp', 'ctx'), 'tp'), may hold values from -0.0625 to 0.0625
Outputs:
- hidden_out: bfloat16 [4096, 2304], P(('fsdp', 'ctx'))
- grad_hidden_in: bfloat16 [4096, 2304], P(('fsdp', 'ctx'))
- grad_pre_attention_gain: float32 [2304], P(('fsdp', 'ctx'))
- grad_post_attention_gain: float32 [2304], P(('fsdp', 'ctx'))
- grad_pre_feedforward_gain: float32 [2304], P(('fsdp', 'ctx'))
- grad_post_feedforward_gain: float32 [2304], P(('fsdp', 'ctx'))
- grad_query_weight: float32 [2304, 2048], P(('fsdp', 'ctx'), 'tp')
- grad_key_weight: float32 [2304, 1024], P(('fsdp', 'ctx'), 'tp')
- grad_value_weight: float32 [2304, 1024], P(('fsdp', 'ctx'), 'tp')
- grad_output_weight: float32 [2304, 2048], P(('fsdp', 'ctx'), 'tp')
- grad_gate_weight: float32 [2304, 9216], P(('fsdp', 'ctx'), 'tp')
- grad_up_weight: float32 [2304, 9216], P(('fsdp', 'ctx'), 'tp')
- grad_down_weight: float32 [2304, 9216], P(('fsdp', 'ctx'), 'tp')
Inputs may be any that keep to these rules, and one draw needn't show every extreme that they name: `segment_ids`: within each group of 1024 tokens document ids increase in order, though some numbers (including 0) may be absent; each begins at a block's start, covers 1 to 4 blocks of 128 tokens with its padding (-1) only at the end of its last block, and never leaves its group; every group holds a document of 512 tokens and a block of padding only among its first 5 blocks.
All inputs are finite; a program needn't handle non-finite values.
Results may differ from a plain program's by a relative error of at most 0.022.
The roundings to bfloat16 on the way count: a program that leaves them out, or rounds other values in their place, can miss the bound.
Values may be sent and summed in bfloat16 or wider, within the bound.
No kernel may reach another device: no remote copies, remote signals or barrier semaphores. Data moves between devices by JAX's collectives and lax.ppermute only.
A program may use at most 256 MiB of HBM per device.

v0:
```python
import jax
import jax.numpy as jnp
from jax import lax
from jax.sharding import PartitionSpec as P

HD = 256
CAP = 50.0
EPS = 1e-06


def passed_along(block, axis, distance):
    devices = range(lax.axis_size(axis))
    route = [(i - distance, i) for i in devices if i - distance in devices]
    return lax.ppermute(block, axis, route)


def rms(value, gain):
    return value * lax.rsqrt(jnp.mean(value * value, axis=-1, keepdims=True) + EPS) * gain


def geglu(gate_value, up_value):
    return jax.nn.gelu(gate_value, approximate=True) * up_value


def product(left, right):
    return jnp.dot(left, right, preferred_element_type=jnp.float32)


def rows_product(left, right):
    return lax.dot_general(
        left, right, (((0,), (0,)), ((), ())), preferred_element_type=jnp.float32
    )


def transposed_product(left, right):
    return lax.dot_general(
        left, right, (((1,), (1,)), ((), ())), preferred_element_type=jnp.float32
    )


def attention_scores(queries, keys_all, allowed, scaling):
    scores = (
        jnp.einsum("qgrd,kgd->grqk", queries, keys_all, preferred_element_type=jnp.float32)
        * scaling
    )
    capped = CAP * jnp.tanh(scores / CAP)
    powers = jnp.where(allowed[None, None], jnp.exp(capped), 0.0)
    return (scores, powers)


def shards(
    hidden_in,
    cotangent,
    segment_ids,
    pre_attention_gain,
    post_attention_gain,
    pre_feedforward_gain,
    post_feedforward_gain,
    query_weight,
    key_weight,
    value_weight,
    output_weight,
    gate_weight,
    up_weight,
    down_weight,
):
    query_full, key_full, value_full, output_full, gate_full, up_full, down_full = (
        lax.all_gather(query_weight, ("fsdp", "ctx"), axis=0, tiled=True),
        lax.all_gather(key_weight, ("fsdp", "ctx"), axis=0, tiled=True),
        lax.all_gather(value_weight, ("fsdp", "ctx"), axis=0, tiled=True),
        lax.all_gather(output_weight, ("fsdp", "ctx"), axis=0, tiled=True),
        lax.all_gather(gate_weight, ("fsdp", "ctx"), axis=0, tiled=True),
        lax.all_gather(up_weight, ("fsdp", "ctx"), axis=0, tiled=True),
        lax.all_gather(down_weight, ("fsdp", "ctx"), axis=0, tiled=True),
    )
    length = hidden_in.shape[0]
    kv_heads = key_weight.shape[1] // HD
    repeats = query_weight.shape[1] // key_weight.shape[1]
    scaling = HD ** (-0.5)
    position = lax.axis_index("ctx")
    own_ids = lax.dynamic_slice_in_dim(segment_ids, position * length, length)
    prev_start = jnp.maximum(position - 1, 0) * length
    prev_ids = jnp.where(
        position > 0, lax.dynamic_slice_in_dim(segment_ids, prev_start, length), -2
    )
    key_ids = jnp.concatenate([prev_ids, own_ids])
    query_pos = jnp.arange(length, dtype=jnp.int32)
    key_pos = jnp.arange(2 * length, dtype=jnp.int32) - length
    allowed = (query_pos[:, None] == key_pos[None, :]) | (own_ids[:, None] == key_ids[None, :]) & (
        own_ids[:, None] >= 0
    ) & (key_pos[None, :] < query_pos[:, None])
    inputs = hidden_in.astype(jnp.float32)
    normed_one = rms(inputs, pre_attention_gain).astype(jnp.bfloat16)
    query_low = product(normed_one, query_full).astype(jnp.bfloat16)
    key_low = product(normed_one, key_full).astype(jnp.bfloat16)
    value_low = product(normed_one, value_full).astype(jnp.bfloat16)
    key_prev, value_prev = passed_along((key_low, value_low), "ctx", 1)
    keys_all = jnp.concatenate([key_prev, key_low], axis=0).reshape(2 * length, kv_heads, HD)
    values_all = jnp.concatenate([value_prev, value_low], axis=0).reshape(2 * length, kv_heads, HD)
    queries = query_low.reshape(length, kv_heads, repeats, HD)
    scores, powers = attention_scores(queries, keys_all, allowed, scaling)
    totals = jnp.sum(powers, axis=-1, keepdims=True)
    probs_low = (powers / totals).astype(jnp.bfloat16)
    attended = jnp.einsum(
        "grqk,kgd->qgrd", probs_low, values_all, preferred_element_type=jnp.float32
    )
    attended_low = attended.reshape(length, -1).astype(jnp.bfloat16)
    branch_one = lax.psum(transposed_product(attended_low, output_full), "tp")
    middle = inputs + rms(branch_one, post_attention_gain)
    normed_two = rms(middle, pre_feedforward_gain).astype(jnp.bfloat16)
    gate_value = product(normed_two, gate_full)
    up_value = product(normed_two, up_full)
    hidden_low = geglu(gate_value, up_value).astype(jnp.bfloat16)
    branch_two = lax.psum(transposed_product(hidden_low, down_full), "tp")
    result = middle + rms(branch_two, post_feedforward_gain)
    upstream = cotangent.astype(jnp.float32)
    query_full, key_full, value_full, output_full, gate_full, up_full, down_full = (
        lax.all_gather(query_weight, ("fsdp", "ctx"), axis=0, tiled=True),
        lax.all_gather(key_weight, ("fsdp", "ctx"), axis=0, tiled=True),
        lax.all_gather(value_weight, ("fsdp", "ctx"), axis=0, tiled=True),
        lax.all_gather(output_weight, ("fsdp", "ctx"), axis=0, tiled=True),
        lax.all_gather(gate_weight, ("fsdp", "ctx"), axis=0, tiled=True),
        lax.all_gather(up_weight, ("fsdp", "ctx"), axis=0, tiled=True),
        lax.all_gather(down_weight, ("fsdp", "ctx"), axis=0, tiled=True),
    )
    unused_four, pull_four = jax.vjp(rms, branch_two, post_feedforward_gain)
    grad_branch_two, grad_gain_four = pull_four(upstream)
    grad_two_low = grad_branch_two.astype(jnp.bfloat16)
    grad_hidden_units = product(grad_two_low, down_full)
    unused_glu, pull_glu = jax.vjp(geglu, gate_value, up_value)
    grad_gate, grad_up = pull_glu(grad_hidden_units)
    grad_gate_low = grad_gate.astype(jnp.bfloat16)
    grad_up_low = grad_up.astype(jnp.bfloat16)
    grad_down_full = rows_product(grad_two_low, hidden_low)
    grad_gate_full = rows_product(normed_two, grad_gate_low)
    grad_up_full = rows_product(normed_two, grad_up_low)
    grad_normed_two = lax.psum(
        transposed_product(grad_gate_low, gate_full) + transposed_product(grad_up_low, up_full),
        "tp",
    )
    unused_three, pull_three = jax.vjp(rms, middle, pre_feedforward_gain)
    grad_middle_norm, grad_gain_three = pull_three(grad_normed_two)
    grad_middle = upstream + grad_middle_norm
    unused_two, pull_two = jax.vjp(rms, branch_one, post_attention_gain)
    grad_branch_one, grad_gain_two = pull_two(grad_middle)
    grad_one_low = grad_branch_one.astype(jnp.bfloat16)
    grad_output_full = rows_product(grad_one_low, attended_low)
    grad_attended = (
        product(grad_one_low, output_full)
        .astype(jnp.bfloat16)
        .reshape(length, kv_heads, repeats, HD)
    )
    scores, powers = attention_scores(queries, keys_all, allowed, scaling)
    probs = powers / totals
    probs_low = probs.astype(jnp.bfloat16)
    grad_probs = jnp.einsum(
        "qgrd,kgd->grqk", grad_attended, values_all, preferred_element_type=jnp.float32
    )
    inner = jnp.sum(probs * grad_probs, axis=-1, keepdims=True)
    grad_capped = probs * (grad_probs - inner)
    squashed = jnp.tanh(scores / CAP)
    grad_scores = (grad_capped * (1.0 - squashed * squashed)).astype(jnp.bfloat16)
    grad_query_low = (
        (
            jnp.einsum("grqk,kgd->qgrd", grad_scores, keys_all, preferred_element_type=jnp.float32)
            * scaling
        )
        .reshape(length, -1)
        .astype(jnp.bfloat16)
    )
    grad_keys_all = (
        jnp.einsum("grqk,qgrd->kgd", grad_scores, queries, preferred_element_type=jnp.float32)
        * scaling
    )
    grad_values_all = jnp.einsum(
        "grqk,qgrd->kgd", probs_low, grad_attended, preferred_element_type=jnp.float32
    )
    grad_key_back, grad_value_back = (
        passed_along(grad_keys_all[:length].astype(jnp.bfloat16), "ctx", -1).astype(jnp.float32),
        passed_along(grad_values_all[:length].astype(jnp.bfloat16), "ctx", -1).astype(jnp.float32),
    )
    grad_key_low = (grad_keys_all[length:] + grad_key_back).reshape(length, -1).astype(jnp.bfloat16)
    grad_value_low = (
        (grad_values_all[length:] + grad_value_back).reshape(length, -1).astype(jnp.bfloat16)
    )
    grad_query_full = rows_product(normed_one, grad_query_low)
    grad_key_full = rows_product(normed_one, grad_key_low)
    grad_value_full = rows_product(normed_one, grad_value_low)
    grad_normed_one = lax.psum(
        (
            transposed_product(grad_query_low, query_full)
            + transposed_product(grad_key_low, key_full)
            + transposed_product(grad_value_low, value_full)
        ).astype(jnp.bfloat16),
        "tp",
    ).astype(jnp.float32)
    unused_one, pull_one = jax.vjp(rms, inputs, pre_attention_gain)
    grad_inputs_norm, grad_gain_one = pull_one(grad_normed_one)
    grad_inputs = grad_middle + grad_inputs_norm
    every_share = tuple(
        (
            lax.psum_scatter(
                grad_query_full.astype(jnp.bfloat16),
                ("fsdp", "ctx"),
                scatter_dimension=0,
                tiled=True,
            ).astype(jnp.float32),
            lax.psum_scatter(
                grad_key_full.astype(jnp.bfloat16), ("fsdp", "ctx"), scatter_dimension=0, tiled=True
            ).astype(jnp.float32),
            lax.psum_scatter(
                grad_value_full.astype(jnp.bfloat16),
                ("fsdp", "ctx"),
                scatter_dimension=0,
                tiled=True,
            ).astype(jnp.float32),
            lax.psum_scatter(
                grad_output_full.astype(jnp.bfloat16),
                ("fsdp", "ctx"),
                scatter_dimension=0,
                tiled=True,
            ).astype(jnp.float32),
            lax.psum_scatter(
                grad_gate_full.astype(jnp.bfloat16),
                ("fsdp", "ctx"),
                scatter_dimension=0,
                tiled=True,
            ).astype(jnp.float32),
            lax.psum_scatter(
                grad_up_full.astype(jnp.bfloat16), ("fsdp", "ctx"), scatter_dimension=0, tiled=True
            ).astype(jnp.float32),
            lax.psum_scatter(
                grad_down_full.astype(jnp.bfloat16),
                ("fsdp", "ctx"),
                scatter_dimension=0,
                tiled=True,
            ).astype(jnp.float32),
            lax.psum_scatter(
                jnp.stack([grad_gain_one, grad_gain_two, grad_gain_three, grad_gain_four]).astype(
                    jnp.bfloat16
                ),
                ("fsdp", "ctx"),
                scatter_dimension=1,
                tiled=True,
            ).astype(jnp.float32),
        )
    )
    gain_shares = every_share[7]
    weight_shares = every_share[:7]
    return (
        result.astype(jnp.bfloat16),
        grad_inputs.astype(jnp.bfloat16),
        gain_shares[0],
        gain_shares[1],
        gain_shares[2],
        gain_shares[3],
    ) + tuple(weight_shares)


def solution(mesh):
    return jax.shard_map(
        shards,
        mesh=mesh,
        in_specs=(
            P(("fsdp", "ctx"), None),
            P(("fsdp", "ctx"), None),
            P("fsdp"),
            P(),
            P(),
            P(),
            P(),
            P(("fsdp", "ctx"), "tp"),
            P(("fsdp", "ctx"), "tp"),
            P(("fsdp", "ctx"), "tp"),
            P(("fsdp", "ctx"), "tp"),
            P(("fsdp", "ctx"), "tp"),
            P(("fsdp", "ctx"), "tp"),
            P(("fsdp", "ctx"), "tp"),
        ),
        out_specs=(
            P(("fsdp", "ctx"), None),
            P(("fsdp", "ctx"), None),
            P(("fsdp", "ctx")),
            P(("fsdp", "ctx")),
            P(("fsdp", "ctx")),
            P(("fsdp", "ctx")),
            P(("fsdp", "ctx"), "tp"),
            P(("fsdp", "ctx"), "tp"),
            P(("fsdp", "ctx"), "tp"),
            P(("fsdp", "ctx"), "tp"),
            P(("fsdp", "ctx"), "tp"),
            P(("fsdp", "ctx"), "tp"),
            P(("fsdp", "ctx"), "tp"),
        ),
        check_vma=False,
    )
```

profile of v0, /device:TPU:0, one launch (start us, length us, event | category | flops | bytes accessed | tf_op | source)
XLA Modules:
  0.0 1507.4 jit_solution(7365926386257940180)
XLA Ops:
  15.4 21.2 %all-gather.8.cloned.1.call-done = bf16[2304,256]{1,0:T(8,128)(2,1)} async-done(((bf16[288,256]{1,0:T(8,128)(2,1)}), bf16[2304,256]{1,0:T(8,128)(2,1)}) %all-gather.8.cloned.1.call-update) | async-done | bytes 1179664 | tf_op jit(solution)/shard_map/all_gather | solution.py:70
  44.1 19.7 %all-gather.10.cloned.1.call-done = bf16[2304,256]{1,0:T(8,128)(2,1)} async-done(((bf16[288,256]{1,0:T(8,128)(2,1)}), bf16[2304,256]{1,0:T(8,128)(2,1)}) %all-gather.10.cloned.1.call-update) | async-done | bytes 1179664 | tf_op jit(solution)/shard_map/all_gather | solution.py:69
  69.4 25.6 %all-gather.12.cloned.1.call-done = bf16[2304,512]{1,0:T(8,128)(2,1)} async-done(((bf16[288,512]{1,0:T(8,128)(2,1)}), bf16[2304,512]{1,0:T(8,128)(2,1)}) %all-gather.12.cloned.1.call-update) | async-done | bytes 2359312 | tf_op jit(solution)/shard_map/all_gather | solution.py:68
  104.7 20.9 %all-gather.14.cloned.1.call-done = bf16[2304,512]{1,0:T(8,128)(2,1)} async-done(((bf16[288,512]{1,0:T(8,128)(2,1)}), bf16[2304,512]{1,0:T(8,128)(2,1)}) %all-gather.14.cloned.1.call-update) | async-done | bytes 2359312 | tf_op jit(solution)/shard_map/all_gather | solution.py:71
  125.6 5.3 fusion.70
  133.3 169.7 %all-reduce.5.cloned.1.call-done = f32[512,2304]{1,0:T(8,128)} async-done(((f32[512,2304]{1,0:T(8,128)}), f32[512,2304]{1,0:T(8,128)}) %all-reduce.5.cloned.1.call-update) | async-done | bytes 4718608 | tf_op jit(solution)/shard_map/psum | solution.py:108
  310.6 56.9 %all-gather.16.cloned.1.call-done = bf16[2304,2304]{1,0:T(8,128)(2,1)} async-done(((bf16[288,2304]{1,0:T(8,128)(2,1)}), bf16[2304,2304]{1,0:T(8,128)(2,1)}) %all-gather.16.cloned.1.call-update) | async-done | bytes 10616848 | tf_op jit(solution)/shard_map/all_gather | solution.py:72
  367.4 11.3 fusion.71
  378.7 54.3 %all-gather.18.cloned.1.call-done = bf16[2304,2304]{1,0:T(8,128)(2,1)} async-done(((bf16[288,2304]{1,0:T(8,128)(2,1)}), bf16[2304,2304]{1,0:T(8,128)(2,1)}) %all-gather.18.cloned.1.call-update) | async-done | bytes 10616848 | tf_op jit(solution)/shard_map/all_gather | solution.py:73
  433.0 12.5 multiply_convert_fusion.1
  445.5 53.1 %all-gather.20.cloned.1.call-done = bf16[2304,2304]{1,0:T(8,128)(2,1)} async-done(((bf16[288,2304]{1,0:T(8,128)(2,1)}), bf16[2304,2304]{1,0:T(8,128)(2,1)}) %all-gather.20.cloned.1.call-update) | async-done | bytes 10616848 | tf_op jit(solution)/shard_map/all_gather | solution.py:74
  498.6 11.7 fusion.72
  510.8 171.7 %all-reduce.7.cloned.1.call-done = f32[512,2304]{1,0:T(8,128)} async-done(((f32[512,2304]{1,0:T(8,128)}), f32[512,2304]{1,0:T(8,128)}) %all-reduce.7.cloned.1.call-update) | async-done | bytes 4718608 | tf_op jit(solution)/shard_map/psum | solution.py:114
  692.8 14.7 multiply_convert_fusion
  707.6 7.3 fusion.73
  714.9 12.4 convolution_add_fusion.2
  727.5 170.9 %all-reduce.9.cloned.1.call-done = f32[512,2304]{1,0:T(8,128)} async-done(((f32[512,2304]{1,0:T(8,128)}), f32[512,2304]{1,0:T(8,128)}) %all-reduce.9.cloned.1.call-update) | async-done | bytes 4718608 | tf_op jit(solution)/shard_map/psum | solution.py:137
  898.4 5.1 multiply_reduce_fusion
  903.5 5.5 multiply_reduce_fusion.1
  928.7 5.3 collective-permute-done.2
  944.4 86.5 %all-reduce.11.cloned.1.call-done = bf16[512,2304]{1,0:T(8,128)(2,1)} async-done(((bf16[512,2304]{1,0:T(8,128)(2,1)}), bf16[512,2304]{1,0:T(8,128)(2,1)}) %all-reduce.11.cloned.1.call-update) | async-done | bytes 2359312 | tf_op jit(solution)/shard_map/psum | solution.py:189
  1043.9 10.3 convolution_convert_fusion.1
  1054.3 10.4 convolution_convert_fusion.2
  1064.7 10.4 convolution_convert_fusion
  1076.8 32.9 %reduce-scatter.13.cloned.1.call-done = bf16[288,256]{1,0:T(8,128)(2,1)} async-done(((bf16[2304,256]{1,0:T(8,128)(2,1)}), bf16[288,256]{1,0:T(8,128)(2,1)}) %reduce-scatter.13.cloned.1.call-update) | async-done | bytes 147472 | tf_op jit(solution)/shard_map/reduce_scatter | solution.py:208
  1111.3 5.9 fusion.18
  1117.2 30.4 %reduce-scatter.25.cloned.1.call-done = bf16[288,4]{1,0:T(8,128)(2,1)} async-done(((bf16[2304,4]{1,0:T(8,128)(2,1)}), bf16[288,4]{1,0:T(8,128)(2,1)}) %reduce-scatter.25.cloned.1.call-update) | async-done | bytes 2320
  1149.2 44.0 %reduce-scatter.17.cloned.1.call-done = bf16[288,512]{1,0:T(8,128)(2,1)} async-done(((bf16[2304,512]{1,0:T(8,128)(2,1)}), bf16[288,512]{1,0:T(8,128)(2,1)}) %reduce-scatter.17.cloned.1.call-update) | async-done | bytes 294928 | tf_op jit(solution)/shard_map/reduce_scatter | solution.py:217
  1195.0 44.3 %reduce-scatter.11.cloned.1.call-done = bf16[288,512]{1,0:T(8,128)(2,1)} async-done(((bf16[2304,512]{1,0:T(8,128)(2,1)}), bf16[288,512]{1,0:T(8,128)(2,1)}) %reduce-scatter.11.cloned.1.call-update) | async-done | bytes 294928 | tf_op jit(solution)/shard_map/reduce_scatter | solution.py:202
  1241.2 84.1 %reduce-scatter.21.cloned.1.call-done = bf16[288,2304]{1,0:T(8,128)(2,1)} async-done(((bf16[2304,2304]{1,0:T(8,128)(2,1)}), bf16[288,2304]{1,0:T(8,128)(2,1)}) %reduce-scatter.21.cloned.1.call-update) | async-done | bytes 1327120 | tf_op jit(solution)/shard_map/reduce_scatter | solution.py:229
  1328.3 83.0 %reduce-scatter.19.cloned.1.call-done = bf16[288,2304]{1,0:T(8,128)(2,1)} async-done(((bf16[2304,2304]{1,0:T(8,128)(2,1)}), bf16[288,2304]{1,0:T(8,128)(2,1)}) %reduce-scatter.19.cloned.1.call-update) | async-done | bytes 1327120 | tf_op jit(solution)/shard_map/reduce_scatter | solution.py:223
  1414.3 83.2 %reduce-scatter.23.cloned.1.call-done = bf16[288,2304]{1,0:T(8,128)(2,1)} async-done(((bf16[2304,2304]{1,0:T(8,128)(2,1)}), bf16[288,2304]{1,0:T(8,128)(2,1)}) %reduce-scatter.23.cloned.1.call-update) | async-done | bytes 1327120 | tf_op jit(solution)/shard_map/reduce_scatter | solution.py:232
  (200 shorter events, 112.0 us)
Async XLA Ops:
  7.2 29.4 %all-gather.8.cloned.1.call-start = ((), (), s32[]{:S(2)}) async-start(), calls=%async_computation.8 | async-start | bytes 1327104 | tf_op jit(solution)/shard_map/all_gather | solution.py:70
  7.9 55.9 %all-gather.10.cloned.1.call-start = ((), (), s32[]{:S(2)}) async-start(), calls=%async_computation.9 | async-start | bytes 1327104 | tf_op jit(solution)/shard_map/all_gather | solution.py:69
  8.7 86.3 %all-gather.12.cloned.1.call-start = ((), (), s32[]{:S(2)}) async-start(), calls=%async_computation.10 | async-start | bytes 2654208 | tf_op jit(solution)/shard_map/all_gather | solution.py:68
  9.4 116.2 %all-gather.14.cloned.1.call-start = ((), (), s32[]{:S(2)}) async-start(), calls=%async_computation.11 | async-start | bytes 2654208 | tf_op jit(solution)/shard_map/all_gather | solution.py:71
  10.0 293.0 %all-reduce.5.cloned.1.call-start = ((), (), s32[]{:S(2)}) async-start(), calls=%async_computation.12 | async-start | bytes 9437184 | tf_op jit(solution)/shard_map/psum | solution.py:108
  13.8 81.2 %copy-start.31 = (f32[512]{0:T(512)}, f32[512]{0:T(512)S(1)}, u32[]{:S(2)}) copy-start(f32[512]{0:T(512)S(1)} %fusion.50) | copy-start | bytes 6148
  15.4 48.5 %copy-start.4 = (bf16[512,2304]{1,0:T(8,128)(2,1)S(1)}, bf16[512,2304]{1,0:T(8,128)(2,1)}, u32[]{:S(2)}) copy-start(bf16[512,2304]{1,0:T(8,128)(2,1)} %param.14) | copy-start | bytes 7077892
  15.4 48.5 %copy-start.29 = (f32[2304]{0:T(1024)S(1)}, f32[2304]{0:T(1024)}, u32[]{:S(2)}) copy-start(f32[2304]{0:T(1024)} %param.17) | copy-start | bytes 27652
  40.1 59.7 %collective-permute-start = (bf16[512,256]{1,0:T(8,128)(2,1)}, bf16[512,256]{1,0:T(8,128)(2,1)}, u32[]{:S(2)}, u32[]{:S(2)}) collective-permute-start(bf16[512,256]{1,0:T(8,128)(2,1)} %convolution_convert_fusion.10), channel_id=1, source_target_pairs={{0,4},{1,5},{2,6},{3,7},{8,12},{9,13},{10,14},{11,15},{16,20},{17,... | collective-permute-start | bytes 786440 | tf_op jit(solution)/shard_map/ppermute | solution.py:14
  66.0 32.2 %collective-permute-start.1 = (bf16[512,256]{1,0:T(8,128)(2,1)S(1)}, bf16[512,256]{1,0:T(8,128)(2,1)S(1)}, u32[]{:S(2)}, u32[]{:S(2)}) collective-permute-start(bf16[512,256]{1,0:T(8,128)(2,1)S(1)} %convolution_convert_fusion.9), channel_id=1, source_target_pairs={{0,4},{1,5},{2,6},{3,7},{8,12},{9,13},{10,14},{11,15},{16,20},{17,... | collective-permute-start | bytes 786440 | tf_op jit(solution)/shard_map/ppermute | solution.py:14
  130.9 175.0 %copy-start.27 = (f32[2304]{0:T(1024)S(1)}, f32[2304]{0:T(1024)}, u32[]{:S(2)}) copy-start(f32[2304]{0:T(1024)} %param.18) | copy-start | bytes 27652
  130.9 236.5 %all-gather.16.cloned.1.call-start = ((), (), s32[]{:S(2)}) async-start(), calls=%async_computation.13 | async-start | bytes 11943936 | tf_op jit(solution)/shard_map/all_gather | solution.py:72
  131.5 301.5 %all-gather.18.cloned.1.call-start = ((), (), s32[]{:S(2)}) async-start(), calls=%async_computation.14 | async-start | bytes 11943936 | tf_op jit(solution)/shard_map/all_gather | solution.py:73
  132.3 366.3 %all-gather.20.cloned.1.call-start = ((), (), s32[]{:S(2)}) async-start(), calls=%async_computation.15 | async-start | bytes 11943936 | tf_op jit(solution)/shard_map/all_gather | solution.py:74
  133.0 549.5 %all-reduce.7.cloned.1.call-start = ((), (), s32[]{:S(2)}) async-start(), calls=%async_computation.16 | async-start | bytes 9437184 | tf_op jit(solution)/shard_map/psum | solution.py:114
  310.5 122.5 %copy-start.12 = (bf16[512,2304]{1,0:T(8,128)(2,1)}, bf16[512,2304]{1,0:T(8,128)(2,1)S(1)}, u32[]{:S(2)}) copy-start(bf16[512,2304]{1,0:T(8,128)(2,1)S(1)} %multiply_convert_fusion.2) | copy-start | bytes 7077892
  510.3 175.0 %copy-start.6 = (bf16[512,2304]{1,0:T(8,128)(2,1)S(1)}, bf16[512,2304]{1,0:T(8,128)(2,1)}, u32[]{:S(2)}) copy-start(bf16[512,2304]{1,0:T(8,128)(2,1)} %param.15) | copy-start | bytes 7077892
  510.3 175.0 %copy-start.28 = (f32[2304]{0:T(1024)S(1)}, f32[2304]{0:T(1024)}, u32[]{:S(2)}) copy-start(f32[2304]{0:T(1024)} %param.20) | copy-start | bytes 27652
  510.4 388.0 %all-reduce.9.cloned.1.call-start = ((), (), s32[]{:S(2)}) async-start(), calls=%async_computation.17 | async-start | bytes 9437184 | tf_op jit(solution)/shard_map/psum | solution.py:137
  727.3 303.7 %all-reduce.11.cloned.1.call-start = ((), (), s32[]{:S(2)}) async-start(), calls=%async_computation.18 | async-start | bytes 4718592 | tf_op jit(solution)/shard_map/psum | solution.py:189
  917.2 17.6 %collective-permute-start.3 = (bf16[512,1,256]{0,2,1:T(8,128)(2,1)S(1)}, bf16[512,1,256]{0,2,1:T(8,128)(2,1)S(1)}, u32[]{:S(2)}, u32[]{:S(2)}) collective-permute-start(bf16[512,1,256]{0,2,1:T(8,128)(2,1)S(1)} %slice.62), channel_id=1, source_target_pairs={{4,0},{5,1},{6,2},{7,3},{12,8},{13,9},{14,10},{15,11},{20,16},{21,... | collective-permute-start | bytes 786440 | tf_op jit(solution)/shard_map/ppermute | solution.py:14
  924.1 9.8 collective-permute-start.2
  937.9 137.3 %reduce-scatter.15.cloned.1.call-start = ((), (), s32[]{:S(2)}) async-start(), calls=%async_computation.21 | async-start | bytes 1327104 | tf_op jit(solution)/shard_map/reduce_scatter | solution.py:211
  941.2 168.5 %reduce-scatter.13.cloned.1.call-start = ((), (), s32[]{:S(2)}) async-start(), calls=%async_computation.20 | async-start | bytes 1327104 | tf_op jit(solution)/shard_map/reduce_scatter | solution.py:208
  944.3 91.5 %copy-start.21 = (bf16[256,2,512]{2,0,1:T(8,128)(2,1)S(1)}, bf16[256,2,512]{2,0,1:T(8,128)(2,1)}, u32[]{:S(2)}) copy-start(bf16[256,2,512]{2,0,1:T(8,128)(2,1)} %copy-done.20) | copy-start | bytes 1572868
  944.3 203.3 %reduce-scatter.25.cloned.1.call-start = ((), (), s32[]{:S(2)}) async-start(), calls=%async_computation.26 | async-start | bytes 663552
  1035.8 157.4 %reduce-scatter.17.cloned.1.call-start = ((), (), s32[]{:S(2)}) async-start(), calls=%async_computation.22 | async-start | bytes 2654208 | tf_op jit(solution)/shard_map/reduce_scatter | solution.py:217
  1040.5 198.8 %reduce-scatter.11.cloned.1.call-start = ((), (), s32[]{:S(2)}) async-start(), calls=%async_computation.19 | async-start | bytes 2654208 | tf_op jit(solution)/shard_map/reduce_scatter | solution.py:202
  1043.6 281.7 %reduce-scatter.21.cloned.1.call-start = ((), (), s32[]{:S(2)}) async-start(), calls=%async_computation.24 | async-start | bytes 11943936 | tf_op jit(solution)/shard_map/reduce_scatter | solution.py:229
  1054.2 357.1 %reduce-scatter.19.cloned.1.call-start = ((), (), s32[]{:S(2)}) async-start(), calls=%async_computation.23 | async-start | bytes 11943936 | tf_op jit(solution)/shard_map/reduce_scatter | solution.py:223
  1064.7 432.8 %reduce-scatter.23.cloned.1.call-start = ((), (), s32[]{:S(2)}) async-start(), calls=%async_computation.25 | async-start | bytes 11943936 | tf_op jit(solution)/shard_map/reduce_scatter | solution.py:232
  1075.1 36.2 %copy-start.34 = (f32[512]{0:T(512)S(1)}, f32[512]{0:T(512)}, u32[]{:S(2)}) copy-start(f32[512]{0:T(512)} %copy-done.33) | copy-start | bytes 6148
  (38 other events, 254.8 us)
Sparse Core Ops, SparseCore 0:
  9.9 26.6 all-gather.7
  38.4 25.3 all-gather.9
  65.7 29.1 all-gather.11
  96.7 28.8 all-gather.13
  131.0 171.9 all-reduce.4
  304.8 62.6 all-gather.15
  369.3 63.6 all-gather.17
  434.9 63.6 all-gather.19
  510.5 171.9 all-reduce.6
  727.4 170.9 all-reduce.8
  938.0 92.8 all-reduce.10
  1034.0 35.6 reduce-scatter.14
  1073.0 36.6 reduce-scatter.12
  1113.2 34.3 reduce-scatter.24
  1150.8 42.3 reduce-scatter.16
  1196.9 42.3 reduce-scatter.10
  1242.7 82.5 reduce-scatter.20
  1328.7 82.5 reduce-scatter.18
  1414.8 82.5 reduce-scatter.22
where the time goes:
time: 1520 us; the launch traced here: 1510 us
  waiting for transfers between devices  1260 us (83%)
  matrix products  145 us (10%)
  other arithmetic  57.6 us (4%)
    psum x1, waiting for transfers between devices, shards(): branch_two = lax.psum(transposed_product(hidden_low, down_full), 'tp')  172 us
    psum x1, waiting for transfers between devices, shards(): lax.psum(transposed_product(grad_gate_low, gate_full) + transposed_produc...  171 us
    psum x1, waiting for transfers between devices, shards(): branch_one = lax.psum(transposed_product(attended_low, output_full), 'tp')  170 us
    psum x1, waiting for transfers between devices, shards(): lax.psum((transposed_product(grad_query_low, query_full) + transposed_pro...  86.5 us
    reduce_scatter x1, waiting for transfers between devices, shards(): lax.psum_scatter(grad_up_full.astype(jnp.bfloat16), ('fsdp', 'ctx'), scat...  84.1 us
    reduce_scatter x1, waiting for transfers between devices, shards(): lax.psum_scatter(grad_down_full.astype(jnp.bfloat16), ('fsdp', 'ctx'), sc...  83.2 us
    reduce_scatter x1, waiting for transfers between devices, shards(): lax.psum_scatter(grad_gate_full.astype(jnp.bfloat16), ('fsdp', 'ctx'), sc...  83 us
    all_gather x1, waiting for transfers between devices, shards(): lax.all_gather(gate_weight, ('fsdp', 'ctx'), axis=0, tiled=True)  56.9 us
  transfers between devices with their start and end apart: 23, of which 19 were waited for; matrix products, arithmetic and copies ran while one was open for 8% of the time, Pallas kernels for 0%

commit v1 on v0

--- a/solution.py
+++ b/solution.py
@@ -186,13 +186,16 @@
     grad_query_full = rows_product(normed_one, grad_query_low)
     grad_key_full = rows_product(normed_one, grad_key_low)
     grad_value_full = rows_product(normed_one, grad_value_low)
-    grad_normed_one = lax.psum(
-        (
-            transposed_product(grad_query_low, query_full)
-            + transposed_product(grad_key_low, key_full)
-            + transposed_product(grad_value_low, value_full)
-        ).astype(jnp.bfloat16),
-        "tp",
+    grad_normed_one = jnp.sum(
+        lax.all_gather(
+            (
+                transposed_product(grad_query_low, query_full)
+                + transposed_product(grad_key_low, key_full)
+                + transposed_product(grad_value_low, value_full)
+            ).astype(jnp.bfloat16),
+            "tp",
+        ),
+        axis=0,
     ).astype(jnp.float32)
     unused_one, pull_one = jax.vjp(rms, inputs, pre_attention_gain)
     grad_inputs_norm, grad_gain_one = pull_one(grad_normed_one)

time: 1520 us -> 1590 us (1.046)
  waiting for transfers between devices: 1260 us -> 1310 us
    all_gather x0 -> x1, waiting for transfers between devices: none -> 166 us  [shards(): lax.all_gather((transposed_product(grad_query_low, query_full) + transpos...]
    psum x1 -> x0, waiting for transfers between devices: 86.5 us -> none  [shards(): lax.psum((transposed_product(grad_query_low, query_full) + transposed_pro...]
    reduce_scatter x1, waiting for transfers between devices: 32.9 us -> 4.32 us  [shards(): lax.psum_scatter(grad_key_full.astype(jnp.bfloat16), ('fsdp', 'ctx'), sca...]
  transfers between devices with their start and end apart: 23 -> 23, of which waited for: 19 -> 20; matrix products, arithmetic and copies ran while one was open for 8% -> 8% of each run, Pallas kernels for 0% -> 0%
where the time goes in v1:
time: 1590 us; the launch traced here: 1580 us
  waiting for transfers between devices  1310 us (82%)
  matrix products  149 us (9%)
  other arithmetic  72.4 us (5%)
  local copies, waits for them, and re-layouts  17.6 us (1%)
    psum x1, waiting for transfers between devices, shards(): branch_two = lax.psum(transposed_product(hidden_low, down_full), 'tp')  172 us
    psum x1, waiting for transfers between devices, shards(): lax.psum(transposed_product(grad_gate_low, gate_full) + transposed_produc...  171 us
    psum x1, waiting for transfers between devices, shards(): branch_one = lax.psum(transposed_product(attended_low, output_full), 'tp')  170 us
    all_gather x1, waiting for transfers between devices, shards(): lax.all_gather((transposed_product(grad_query_low, query_full) + transpos...  166 us
    reduce_scatter x1, waiting for transfers between devices, shards(): lax.psum_scatter(grad_up_full.astype(jnp.bfloat16), ('fsdp', 'ctx'), scat...  84.1 us
    reduce_scatter x1, waiting for transfers between devices, shards(): lax.psum_scatter(grad_down_full.astype(jnp.bfloat16), ('fsdp', 'ctx'), sc...  83 us
    reduce_scatter x1, waiting for transfers between devices, shards(): lax.psum_scatter(grad_gate_full.astype(jnp.bfloat16), ('fsdp', 'ctx'), sc...  83 us
    all_gather x1, waiting for transfers between devices, shards(): lax.all_gather(gate_weight, ('fsdp', 'ctx'), axis=0, tiled=True)  55.5 us
  transfers between devices with their start and end apart: 23, of which 20 were waited for; matrix products, arithmetic and copies ran while one was open for 8% of the time, Pallas kernels for 0%

profile of v1, /device:TPU:0, one launch (start us, length us, event | category | flops | bytes accessed | tf_op | source)
XLA Modules:
  0.0 1580.4 jit_solution(5570554493173263295)
XLA Ops:
  15.4 21.2 %all-gather.10.cloned.1.call-done = bf16[2304,256]{1,0:T(8,128)(2,1)} async-done(((bf16[288,256]{1,0:T(8,128)(2,1)}), bf16[2304,256]{1,0:T(8,128)(2,1)}) %all-gather.10.cloned.1.call-update) | async-done | bytes 1179664 | tf_op jit(solution)/shard_map/all_gather | solution.py:70
  44.2 19.7 %all-gather.12.cloned.1.call-done = bf16[2304,256]{1,0:T(8,128)(2,1)} async-done(((bf16[288,256]{1,0:T(8,128)(2,1)}), bf16[2304,256]{1,0:T(8,128)(2,1)}) %all-gather.12.cloned.1.call-update) | async-done | bytes 1179664 | tf_op jit(solution)/shard_map/all_gather | solution.py:69
  69.4 25.6 %all-gather.14.cloned.1.call-done = bf16[2304,512]{1,0:T(8,128)(2,1)} async-done(((bf16[288,512]{1,0:T(8,128)(2,1)}), bf16[2304,512]{1,0:T(8,128)(2,1)}) %all-gather.14.cloned.1.call-update) | async-done | bytes 2359312 | tf_op jit(solution)/shard_map/all_gather | solution.py:68
  104.7 21.0 %all-gather.16.cloned.1.call-done = bf16[2304,512]{1,0:T(8,128)(2,1)} async-done(((bf16[288,512]{1,0:T(8,128)(2,1)}), bf16[2304,512]{1,0:T(8,128)(2,1)}) %all-gather.16.cloned.1.call-update) | async-done | bytes 2359312 | tf_op jit(solution)/shard_map/all_gather | solution.py:71
  125.6 5.2 fusion.70
  133.2 169.7 %all-reduce.4.cloned.1.call-done = f32[512,2304]{1,0:T(8,128)} async-done(((f32[512,2304]{1,0:T(8,128)}), f32[512,2304]{1,0:T(8,128)}) %all-reduce.4.cloned.1.call-update) | async-done | bytes 4718608 | tf_op jit(solution)/shard_map/psum | solution.py:108
  311.8 55.5 %all-gather.18.cloned.1.call-done = bf16[2304,2304]{1,0:T(8,128)(2,1)} async-done(((bf16[288,2304]{1,0:T(8,128)(2,1)}), bf16[2304,2304]{1,0:T(8,128)(2,1)}) %all-gather.18.cloned.1.call-update) | async-done | bytes 10616848 | tf_op jit(solution)/shard_map/all_gather | solution.py:72
  367.4 11.6 fusion.71
  379.0 54.0 %all-gather.20.cloned.1.call-done = bf16[2304,2304]{1,0:T(8,128)(2,1)} async-done(((bf16[288,2304]{1,0:T(8,128)(2,1)}), bf16[2304,2304]{1,0:T(8,128)(2,1)}) %all-gather.20.cloned.1.call-update) | async-done | bytes 10616848 | tf_op jit(solution)/shard_map/all_gather | solution.py:73
  433.0 12.8 multiply_convert_fusion.1
  445.8 52.8 %all-gather.22.cloned.1.call-done = bf16[2304,2304]{1,0:T(8,128)(2,1)} async-done(((bf16[288,2304]{1,0:T(8,128)(2,1)}), bf16[2304,2304]{1,0:T(8,128)(2,1)}) %all-gather.22.cloned.1.call-update) | async-done | bytes 10616848 | tf_op jit(solution)/shard_map/all_gather | solution.py:74
  498.5 11.7 fusion.72
  510.8 171.7 %all-reduce.6.cloned.1.call-done = f32[512,2304]{1,0:T(8,128)} async-done(((f32[512,2304]{1,0:T(8,128)}), f32[512,2304]{1,0:T(8,128)}) %all-reduce.6.cloned.1.call-update) | async-done | bytes 4718608 | tf_op jit(solution)/shard_map/psum | solution.py:114
  690.2 5.1 fusion.15
  695.4 14.7 multiply_convert_fusion
  710.2 7.3 fusion.73
  717.5 12.4 convolution_add_fusion.2
  730.1 170.8 %all-reduce.8.cloned.1.call-done = f32[512,2304]{1,0:T(8,128)} async-done(((f32[512,2304]{1,0:T(8,128)}), f32[512,2304]{1,0:T(8,128)}) %all-reduce.8.cloned.1.call-update) | async-done | bytes 4718608 | tf_op jit(solution)/shard_map/psum | solution.py:137
  906.1 6.5 multiply_reduce_fusion.1
  941.7 7.4 collective-permute-done.2
  963.2 10.3 convolution_convert_fusion.1
  973.6 10.4 convolution_convert_fusion.2
  984.3 10.4 convolution_convert_fusion
  1010.1 44.1 %reduce-scatter.17.cloned.1.call-done = bf16[288,512]{1,0:T(8,128)(2,1)} async-done(((bf16[2304,512]{1,0:T(8,128)(2,1)}), bf16[288,512]{1,0:T(8,128)(2,1)}) %reduce-scatter.17.cloned.1.call-update) | async-done | bytes 294928 | tf_op jit(solution)/shard_map/reduce_scatter | solution.py:220
  1056.0 44.3 %reduce-scatter.11.cloned.1.call-done = bf16[288,512]{1,0:T(8,128)(2,1)} async-done(((bf16[2304,512]{1,0:T(8,128)(2,1)}), bf16[288,512]{1,0:T(8,128)(2,1)}) %reduce-scatter.11.cloned.1.call-update) | async-done | bytes 294928 | tf_op jit(solution)/shard_map/reduce_scatter | solution.py:205
  1102.2 84.1 %reduce-scatter.21.cloned.1.call-done = bf16[288,2304]{1,0:T(8,128)(2,1)} async-done(((bf16[2304,2304]{1,0:T(8,128)(2,1)}), bf16[288,2304]{1,0:T(8,128)(2,1)}) %reduce-scatter.21.cloned.1.call-update) | async-done | bytes 1327120 | tf_op jit(solution)/shard_map/reduce_scatter | solution.py:232
  1189.3 83.0 %reduce-scatter.19.cloned.1.call-done = bf16[288,2304]{1,0:T(8,128)(2,1)} async-done(((bf16[2304,2304]{1,0:T(8,128)(2,1)}), bf16[288,2304]{1,0:T(8,128)(2,1)}) %reduce-scatter.19.cloned.1.call-update) | async-done | bytes 1327120 | tf_op jit(solution)/shard_map/reduce_scatter | solution.py:226
  1275.3 83.0 %reduce-scatter.23.cloned.1.call-done = bf16[288,2304]{1,0:T(8,128)(2,1)} async-done(((bf16[2304,2304]{1,0:T(8,128)(2,1)}), bf16[288,2304]{1,0:T(8,128)(2,1)}) %reduce-scatter.23.cloned.1.call-update) | async-done | bytes 1327120 | tf_op jit(solution)/shard_map/reduce_scatter | solution.py:235
  1361.3 165.8 %all-gather.24.cloned.1.call-done = bf16[2048,2304]{1,0:T(8,128)(2,1)} async-done(((bf16[512,2304]{1,0:T(8,128)(2,1)}), bf16[2048,2304]{1,0:T(8,128)(2,1)}) %all-gather.24.cloned.1.call-update) | async-done | bytes 9437200 | tf_op jit(solution)/shard_map/all_gather | solution.py:190
  1527.1 7.1 reduce_sum.153
  1539.1 5.9 fusion.18
  1545.0 26.8 %reduce-scatter.25.cloned.1.call-done = bf16[288,4]{1,0:T(8,128)(2,1)} async-done(((bf16[2304,4]{1,0:T(8,128)(2,1)}), bf16[288,4]{1,0:T(8,128)(2,1)}) %reduce-scatter.25.cloned.1.call-update) | async-done | bytes 2320
  (197 shorter events, 133.3 us)
Async XLA Ops:
  7.2 29.4 %all-gather.10.cloned.1.call-start = ((), (), s32[]{:S(2)}) async-start(), calls=%async_computation.8 | async-start | bytes 1327104 | tf_op jit(solution)/shard_map/all_gather | solution.py:70
  7.9 55.9 %all-gather.12.cloned.1.call-start = ((), (), s32[]{:S(2)}) async-start(), calls=%async_computation.9 | async-start | bytes 1327104 | tf_op jit(solution)/shard_map/all_gather | solution.py:69
  8.7 86.3 %all-gather.14.cloned.1.call-start = ((), (), s32[]{:S(2)}) async-start(), calls=%async_computation.10 | async-start | bytes 2654208 | tf_op jit(solution)/shard_map/all_gather | solution.py:68
  9.4 116.2 %all-gather.16.cloned.1.call-start = ((), (), s32[]{:S(2)}) async-start(), calls=%async_computation.11 | async-start | bytes 2654208 | tf_op jit(solution)/shard_map/all_gather | solution.py:71
  10.0 293.0 %all-reduce.4.cloned.1.call-start = ((), (), s32[]{:S(2)}) async-start(), calls=%async_computation.12 | async-start | bytes 9437184 | tf_op jit(solution)/shard_map/psum | solution.py:108
  13.8 81.2 %copy-start.31 = (f32[512]{0:T(512)}, f32[512]{0:T(512)S(1)}, u32[]{:S(2)}) copy-start(f32[512]{0:T(512)S(1)} %fusion.50) | copy-start | bytes 6148
  15.4 48.5 %copy-start.4 = (bf16[512,2304]{1,0:T(8,128)(2,1)S(1)}, bf16[512,2304]{1,0:T(8,128)(2,1)}, u32[]{:S(2)}) copy-start(bf16[512,2304]{1,0:T(8,128)(2,1)} %param.14) | copy-start | bytes 7077892
  15.4 48.5 %copy-start.28 = (f32[2304]{0:T(1024)S(1)}, f32[2304]{0:T(1024)}, u32[]{:S(2)}) copy-start(f32[2304]{0:T(1024)} %param.17) | copy-start | bytes 27652
  40.1 59.7 %collective-permute-start = (bf16[512,256]{1,0:T(8,128)(2,1)}, bf16[512,256]{1,0:T(8,128)(2,1)}, u32[]{:S(2)}, u32[]{:S(2)}) collective-permute-start(bf16[512,256]{1,0:T(8,128)(2,1)} %convolution_convert_fusion.10), channel_id=1, source_target_pairs={{0,4},{1,5},{2,6},{3,7},{8,12},{9,13},{10,14},{11,15},{16,20},{17,... | collective-permute-start | bytes 786440 | tf_op jit(solution)/shard_map/ppermute | solution.py:14
  66.0 32.2 %copy-start.35 = (bf16[512,256]{1,0:T(8,128)(2,1)}, bf16[512,256]{1,0:T(8,128)(2,1)S(1)}, u32[]{:S(2)}) copy-start(bf16[512,256]{1,0:T(8,128)(2,1)S(1)} %convolution_convert_fusion.9) | copy-start | bytes 786436
  66.0 32.2 %collective-permute-start.1 = (bf16[512,256]{1,0:T(8,128)(2,1)S(1)}, bf16[512,256]{1,0:T(8,128)(2,1)S(1)}, u32[]{:S(2)}, u32[]{:S(2)}) collective-permute-start(bf16[512,256]{1,0:T(8,128)(2,1)S(1)} %convolution_convert_fusion.9), channel_id=1, source_target_pairs={{0,4},{1,5},{2,6},{3,7},{8,12},{9,13},{10,14},{11,15},{16,20},{17,... | collective-permute-start | bytes 786440 | tf_op jit(solution)/shard_map/ppermute | solution.py:14
  104.7 26.2 %copy-start.19 = (bf16[256,2,512]{2,0,1:T(8,128)(2,1)}, bf16[256,2,512]{2,0,1:T(8,128)(2,1)S(1)}, u32[]{:S(2)}) copy-start(bf16[256,2,512]{2,0,1:T(8,128)(2,1)S(1)} %fusion.40) | copy-start | bytes 1572868
  130.9 175.0 %copy-start.26 = (f32[2304]{0:T(1024)S(1)}, f32[2304]{0:T(1024)}, u32[]{:S(2)}) copy-start(f32[2304]{0:T(1024)} %param.18) | copy-start | bytes 27652
  130.9 236.5 %all-gather.18.cloned.1.call-start = ((), (), s32[]{:S(2)}) async-start(), calls=%async_computation.13 | async-start | bytes 11943936 | tf_op jit(solution)/shard_map/all_gather | solution.py:72
  131.5 301.5 %all-gather.20.cloned.1.call-start = ((), (), s32[]{:S(2)}) async-start(), calls=%async_computation.14 | async-start | bytes 11943936 | tf_op jit(solution)/shard_map/all_gather | solution.py:73
  132.2 366.3 %all-gather.22.cloned.1.call-start = ((), (), s32[]{:S(2)}) async-start(), calls=%async_computation.15 | async-start | bytes 11943936 | tf_op jit(solution)/shard_map/all_gather | solution.py:74
  133.0 549.5 %all-reduce.6.cloned.1.call-start = ((), (), s32[]{:S(2)}) async-start(), calls=%async_computation.16 | async-start | bytes 9437184 | tf_op jit(solution)/shard_map/psum | solution.py:114
  510.3 175.0 %copy-start.27 = (f32[2304]{0:T(1024)S(1)}, f32[2304]{0:T(1024)}, u32[]{:S(2)}) copy-start(f32[2304]{0:T(1024)} %param.20) | copy-start | bytes 27652
  510.3 390.6 %all-reduce.8.cloned.1.call-start = ((), (), s32[]{:S(2)}) async-start(), calls=%async_computation.17 | async-start | bytes 9437184 | tf_op jit(solution)/shard_map/psum | solution.py:137
  690.2 19.9 %slice-start.2 = ((s8[10616832]{0:T(1024)(128)(4,1)}), s8[4194304]{0:T(1024)(128)(4,1)S(1)}, s32[]{:S(2)}) async-start(s8[10616832]{0:T(1024)(128)(4,1)} %bitcast.153), calls=%async_computation.29 | async-start | bytes 8388608
  695.3 14.8 copy-start.10
  729.9 272.6 %reduce-scatter.15.cloned.1.call-start = ((), (), s32[]{:S(2)}) async-start(), calls=%async_computation.20 | async-start | bytes 1327104 | tf_op jit(solution)/shard_map/reduce_scatter | solution.py:214
  920.8 9.9 collective-permute-start.3
  933.5 74.9 %reduce-scatter.13.cloned.1.call-start = ((), (), s32[]{:S(2)}) async-start(), calls=%async_computation.19 | async-start | bytes 1327104 | tf_op jit(solution)/shard_map/reduce_scatter | solution.py:211
  940.2 8.9 collective-permute-start.2
  952.0 102.2 %reduce-scatter.17.cloned.1.call-start = ((), (), s32[]{:S(2)}) async-start(), calls=%async_computation.21 | async-start | bytes 2654208 | tf_op jit(solution)/shard_map/reduce_scatter | solution.py:220
  956.7 143.6 %reduce-scatter.11.cloned.1.call-start = ((), (), s32[]{:S(2)}) async-start(), calls=%async_computation.18 | async-start | bytes 2654208 | tf_op jit(solution)/shard_map/reduce_scatter | solution.py:205
  963.1 223.2 %reduce-scatter.21.cloned.1.call-start = ((), (), s32[]{:S(2)}) async-start(), calls=%async_computation.23 | async-start | bytes 11943936 | tf_op jit(solution)/shard_map/reduce_scatter | solution.py:232
  973.5 298.8 %reduce-scatter.19.cloned.1.call-start = ((), (), s32[]{:S(2)}) async-start(), calls=%async_computation.22 | async-start | bytes 11943936 | tf_op jit(solution)/shard_map/reduce_scatter | solution.py:226
  984.0 374.3 %reduce-scatter.23.cloned.1.call-start = ((), (), s32[]{:S(2)}) async-start(), calls=%async_computation.24 | async-start | bytes 11943936 | tf_op jit(solution)/shard_map/reduce_scatter | solution.py:235
  994.7 532.4 %all-gather.24.cloned.1.call-start = ((), (), s32[]{:S(2)}) async-start(), calls=%async_computation.25 | async-start | bytes 11796480 | tf_op jit(solution)/shard_map/all_gather | solution.py:190
  1002.0 569.7 %reduce-scatter.25.cloned.1.call-start = ((), (), s32[]{:S(2)}) async-start(), calls=%async_computation.26 | async-start | bytes 663552
  (36 other events, 166.7 us)
Sparse Core Ops, SparseCore 0:
  9.9 26.6 all-gather.9
  38.4 25.3 all-gather.11
  65.7 29.1 all-gather.13
  96.7 28.8 all-gather.15
  131.0 171.9 all-reduce.3
  304.7 62.6 all-gather.17
  369.2 63.6 all-gather.19
  434.8 63.6 all-gather.21
  510.4 171.9 all-reduce.5
  730.0 170.8 all-reduce.7
  933.7 34.9 reduce-scatter.14
  971.7 36.6 reduce-scatter.12
  1011.8 42.3 reduce-scatter.16
  1057.9 42.3 reduce-scatter.10
  1103.7 82.5 reduce-scatter.20
  1189.7 82.5 reduce-scatter.18
  1275.7 82.5 reduce-scatter.22
  1360.3 166.7 all-gather.23
  1539.2 32.5 reduce-scatter.24
